TPU v7x, 32 devices: a whole 2x2x4 slice. The times are simulated.
32 devices in a mesh: row: 8 (over z, y), col: 2 (over x), fiber: 2 (over core).
Axes of the slice: x: 2, y: 2, z: 4, core: 2. Of those that a mesh axis runs over, the one named last changes fastest.
Arguments:
- a_panels: float32 [3072, 2, 2, 768], P(('row', 'col'), 'fiber'), may hold values from -12 to 12
- b_panels: float32 [2, 2, 768, 2048], P('fiber', None, 'row', 'col'), may hold values from -0.15625 to 0.15625
- a_pattern: int32 [24, 2, 2, 6], P('row', 'fiber'), may hold values 0 or 1
- c_pattern: int32 [24, 16], P('row', 'col'), may hold values 0 or 1
Outputs:
- scaled: float32 [3072, 2048], P(('row', 'fiber'), 'col')
All inputs are finite; a program needn't handle non-finite values. No bound on the sum of `a_pattern` or of `c_pattern` on one device may be relied on, other than what follows from the above.
Results may differ from a plain program's by a relative error of at most 0.00013.
Values sent between devices are 32-bit elements; how exact they have to be, the bound alone decides.
No kernel may reach another device: no remote copies, remote signals or barrier semaphores. Data moves between devices by JAX's collectives and lax.ppermute only.
A program may use at most 64 MiB of HBM per device.

v0:
```python
import jax
import jax.numpy as jnp
from jax import lax
from jax.sharding import PartitionSpec as P

BLK = 128
EPS = 1e-06


def local(a_panels, b_panels, a_pattern, c_pattern):
    block_size = BLK
    section_count = a_panels.shape[2]
    panel_width = a_panels.shape[3]
    block_rows = a_pattern.shape[0]
    width_blocks = a_pattern.shape[3]
    local_rows = block_rows * block_size
    column_count = b_panels.shape[3]
    running_sum = jnp.zeros((local_rows, column_count), jnp.float32)
    for section_index in range(section_count):
        row_block = lax.all_gather(a_panels[:, 0, section_index, :], "col", axis=0, tiled=True)
        keep_left = a_pattern[:, 0, section_index, :].astype(jnp.float32)
        left_panel = (
            row_block.reshape(block_rows, block_size, width_blocks, block_size)
            * keep_left[:, None, :, None]
        ).reshape(local_rows, panel_width)
        right_panel = lax.all_gather(b_panels[0, section_index], "row", axis=0, tiled=True)
        running_sum = running_sum + jnp.dot(
            left_panel,
            right_panel,
            precision=lax.Precision.HIGHEST,
            preferred_element_type=jnp.float32,
        )
    layer_index = lax.axis_index("fiber")
    fibers = lax.axis_size("fiber")
    share_rows = local_rows // fibers
    keep_product = c_pattern.astype(jnp.float32)
    keep_full = jnp.broadcast_to(
        keep_product[:, None, :, None], (block_rows, block_size, keep_product.shape[1], block_size)
    ).reshape(local_rows, column_count)
    merged = lax.psum_scatter(running_sum, "fiber", scatter_dimension=0, tiled=True)
    keep_share = lax.dynamic_slice_in_dim(keep_full, layer_index * share_rows, share_rows, 0)
    product = merged * keep_share
    inflated = product * product
    totals = lax.psum(jnp.sum(inflated, axis=0), ("row", "fiber"))
    row_count = share_rows * lax.axis_size("row") * fibers
    return inflated / (totals / row_count + EPS)


def solution(mesh):
    placed = (
        P(("row", "col"), "fiber", None, None),
        P("fiber", None, "row", "col"),
        P("row", "fiber", None, None),
        P("row", "col"),
    )
    return jax.shard_map(
        local, mesh=mesh, in_specs=placed, out_specs=P(("row", "fiber"), "col"), check_vma=False
    )
```

profile of v0, /device:TPU:0, one launch (start us, length us, event | category | flops | bytes accessed | tf_op | source)
XLA Modules:
  0.0 241.1 jit_solution(13269795928993399024)
XLA Ops:
  6.5 2.8 %fusion.12 = (f32[192,1,1,768]{3,2,1,0:T(1,128)S(1)}, f32[192,1,1,768]{3,2,1,0:T(1,128)S(1)}) fusion(f32[192,1,2,768]{3,2,1,0:T(2,128)} %param.4), kind=kLoop, calls=%fused_computation.20 | loop fusion | bytes 2359296 | tf_op jit(solution)/shard_map/slice | solution.py:20
  9.3 0.9 copy.10
  10.2 0.0 all-gather.15.cloned.1.call-start
  10.2 0.9 fusion.13
  11.2 0.0 all-gather.9.cloned.1.call-start
  11.3 0.9 copy.9
  12.2 0.0 all-gather.11.cloned.1.call-start
  12.3 0.5 all-gather.11.cloned.1.call-update
  12.8 0.0 reduce-scatter.2.cloned.1.call-start
  12.9 23.0 %all-gather.13.cloned.1.call-done = f32[384,1,1,768]{3,0,2,1:T(8,128)} async-done(((f32[192,1,1,768]{3,0,2,1:T(8,128)}), f32[384,1,1,768]{3,0,2,1:T(8,128)}) %all-gather.13.cloned.1.call-update) | async-done | bytes 1179664 | tf_op jit(solution)/shard_map/all_gather | solution.py:20
  35.8 62.2 %all-gather.15.cloned.1.call-done = f32[1,1,768,1024]{3,2,1,0:T(8,128)} async-done(((f32[1,1,96,1024]{3,2,1,0:T(8,128)}), f32[1,1,768,1024]{3,2,1,0:T(8,128)}) %all-gather.15.cloned.1.call-update) | async-done | bytes 3145744 | tf_op jit(solution)/shard_map/all_gather | solution.py:26
  98.1 0.2 mul.34
  98.2 5.9 %fusion = f32[384,1024]{1,0:T(8,128)S(1)} fusion(f32[1,1,768,1024]{3,2,1,0:T(8,128)} %all-gather.15.cloned.1.call-done, f32[48,8,6,128]{3,2,1,0:T(8,128)S(1)} %bitcast.40, f32[384,1,1,768]{3,0,2,1:T(8,128)S(1)} %copy-done.1), kind=kOutput, calls=%fused_computation | convolution fusion | flops 3624173568 | bytes 7077888 | tf_op jit(solution)/shard_map/dot_general | solution.py:27
  104.2 16.9 %all-gather.9.cloned.1.call-done = f32[384,1,1,768]{3,0,2,1:T(8,128)} async-done(((f32[192,1,1,768]{3,0,2,1:T(8,128)}), f32[384,1,1,768]{3,0,2,1:T(8,128)}) %all-gather.9.cloned.1.call-update) | async-done | bytes 1179664 | tf_op jit(solution)/shard_map/all_gather | solution.py:20
  121.1 62.1 %all-gather.11.cloned.1.call-done = f32[1,1,768,1024]{3,2,1,0:T(8,128)} async-done(((f32[1,1,96,1024]{3,2,1,0:T(8,128)}), f32[1,1,768,1024]{3,2,1,0:T(8,128)}) %all-gather.11.cloned.1.call-update) | async-done | bytes 3145744 | tf_op jit(solution)/shard_map/all_gather | solution.py:26
  183.1 0.2 mul.31
  183.3 7.1 %fusion.4 = f32[384,1024]{1,0:T(8,128)} fusion(f32[384,1024]{1,0:T(8,128)S(1)} %fusion, f32[1,1,768,1024]{3,2,1,0:T(8,128)} %all-gather.11.cloned.1.call-done, f32[48,8,6,128]{3,2,1,0:T(8,128)S(1)} %bitcast.41, f32[384,1,1,768]{3,0,2,1:T(8,128)S(1)} %copy-done.2), kind=kOutput, calls=%fused_computation.5 | convolution fusion | flops 3624566784 | bytes 8650752 | tf_op jit(solution)/shard_map/dot_general | solution.py:27
  190.5 0.7 copy-done.5
  191.1 0.2 broadcast_in_dim.2
  191.3 0.3 copy.25
  191.6 6.7 %reduce-scatter.2.cloned.1.call-done = f32[192,1024]{1,0:T(8,128)} async-done(((f32[384,1024]{1,0:T(8,128)}), f32[192,1024]{1,0:T(8,128)}) %reduce-scatter.2.cloned.1.call-update) | async-done | bytes 786448 | tf_op jit(solution)/shard_map/reduce_scatter | solution.py:40
  198.3 1.3 fusion.11
  199.6 33.9 %psum.7 = f32[1024]{0:T(1024)S(1)} all-reduce(f32[1024]{0:T(1024)S(1)} %fusion.11), channel_id=1, replica_groups=mesh['row'=8,'col'=2,'fiber'=2] {'row','fiber'}, use_global_device_ids=true, to_apply=%region_2.0 | all-reduce | flops 1024 | bytes 8192 | tf_op jit(solution)/shard_map/psum | solution.py:44
  233.5 1.0 broadcast_divide_fusion
  (20 shorter events, 0.1 us)
Async XLA Ops:
  6.5 3.7 %copy-start.3 = (f32[1,2,96,1024]{3,2,1,0:T(8,128)S(1)}, f32[1,2,96,1024]{3,2,1,0:T(8,128)}, u32[]{:S(2)}) copy-start(f32[1,2,96,1024]{3,2,1,0:T(8,128)} %param.5) | copy-start | bytes 2359300
  6.5 29.3 %all-gather.13.cloned.1.call-start = ((), (), s32[]{:S(2)}) async-start(), calls=%async_computation.4 | async-start | bytes 1769472 | tf_op jit(solution)/shard_map/all_gather | solution.py:20
  10.2 87.9 %all-gather.15.cloned.1.call-start = ((), (), s32[]{:S(2)}) async-start(), calls=%async_computation.5 | async-start | bytes 3538944 | tf_op jit(solution)/shard_map/all_gather | solution.py:26
  11.2 1.7 copy-start.4
  11.2 109.8 %all-gather.9.cloned.1.call-start = ((), (), s32[]{:S(2)}) async-start(), calls=%async_computation.2 | async-start | bytes 1769472 | tf_op jit(solution)/shard_map/all_gather | solution.py:20
  12.2 170.9 %all-gather.11.cloned.1.call-start = ((), (), s32[]{:S(2)}) async-start(), calls=%async_computation.3 | async-start | bytes 3538944 | tf_op jit(solution)/shard_map/all_gather | solution.py:26
  12.8 185.5 %reduce-scatter.2.cloned.1.call-start = ((), (), s32[]{:S(2)}) async-start(), calls=%async_computation.1 | async-start | bytes 2359296 | tf_op jit(solution)/shard_map/reduce_scatter | solution.py:40
  35.8 62.4 %copy-start.1 = (f32[384,1,1,768]{3,0,2,1:T(8,128)S(1)}, f32[384,1,1,768]{3,0,2,1:T(8,128)}, u32[]{:S(2)}) copy-start(f32[384,1,1,768]{3,0,2,1:T(8,128)} %all-gather.13.cloned.1.call-done) | copy-start | bytes 3538948
  121.1 62.3 %copy-start.2 = (f32[384,1,1,768]{3,0,2,1:T(8,128)S(1)}, f32[384,1,1,768]{3,0,2,1:T(8,128)}, u32[]{:S(2)}) copy-start(f32[384,1,1,768]{3,0,2,1:T(8,128)} %all-gather.9.cloned.1.call-done) | copy-start | bytes 3538948
  190.4 0.7 copy-start.5
  198.3 35.2 %copy-start = (f32[192,1024]{1,0:T(8,128)S(1)}, f32[192,1024]{1,0:T(8,128)}, u32[]{:S(2)}) copy-start(f32[192,1024]{1,0:T(8,128)} %reduce-scatter.2.cloned.1.call-done) | copy-start | bytes 2359300
Sparse Core Ops, SparseCore 0:
  10.3 25.4 all-gather.12
  38.0 60.0 all-gather.14
  99.6 21.4 all-gather.8
  123.1 60.0 all-gather.10
  190.6 7.6 reduce-scatter.1
where the time goes:
time: 241 us
  waiting for transfers between devices  171 us (71%)
  blocking collectives  33.9 us (14%)
  between operations  13.2 us (5%)
  matrix products  13 us (5%)
  local copies, waits for them, and re-layouts  6.99 us (3%)
    all_gather x2, waiting for transfers between devices, local(): lax.all_gather(b_panels[0, section_index], 'row', axis=0, tiled=True)  124 us
    all_gather x2, waiting for transfers between devices, local(): lax.all_gather(a_panels[:, 0, section_index, :], 'col', axis=0, tiled=True)  39.8 us
    psum x1, blocking collectives, local(): totals = lax.psum(jnp.sum(inflated, axis=0), ('row', 'fiber'))  33.9 us
    dot_general x2, matrix products, local(): jnp.dot(left_panel, right_panel, precision=lax.Precision.HIGHEST, preferr...  13 us
    reduce_scatter x1, waiting for transfers between devices, local(): lax.psum_scatter(running_sum, 'fiber', scatter_dimension=0, tiled=True)  6.67 us
  transfers between devices with their start and end apart: 5, of which 5 were waited for; matrix products, arithmetic and copies ran while one was open for 4% of the time, Pallas kernels for 0%

commit v1 on v0

--- a/solution.py
+++ b/solution.py
@@ -41,7 +41,8 @@
     keep_share = lax.dynamic_slice_in_dim(keep_full, layer_index * share_rows, share_rows, 0)
     product = merged * keep_share
     inflated = product * product
-    totals = lax.psum(jnp.sum(inflated, axis=0), ("row", "fiber"))
+    sheet = jnp.sum(inflated, axis=0)
+    totals = jax.lax.all_gather(sheet, axis_name=("row", "fiber")).sum(axis=0)
     row_count = share_rows * lax.axis_size("row") * fibers
     return inflated / (totals / row_count + EPS)
 

time: 241 us -> 229 us (0.950)
  blocking collectives: 33.9 us -> 21.9 us
    psum x1 -> x0, blocking collectives: 33.9 us -> none  [local(): totals = lax.psum(jnp.sum(inflated, axis=0), ('row', 'fiber'))]
    all_gather x0 -> x1, blocking collectives: none -> 21.9 us  [local(): totals = jax.lax.all_gather(sheet, axis_name=('row', 'fiber')).sum(axis=0)]
where the time goes in v1:
time: 229 us
  waiting for transfers between devices  171 us (75%)
  blocking collectives  21.9 us (10%)
  between operations  13.3 us (6%)
  matrix products  13 us (6%)
  local copies, waits for them, and re-layouts  7.01 us (3%)
  other arithmetic  2.38 us (1%)
    all_gather x2, waiting for transfers between devices, local(): lax.all_gather(b_panels[0, section_index], 'row', axis=0, tiled=True)  124 us
    all_gather x2, waiting for transfers between devices, local(): lax.all_gather(a_panels[:, 0, section_index, :], 'col', axis=0, tiled=True)  39.8 us
    all_gather x1, blocking collectives, local(): totals = jax.lax.all_gather(sheet, axis_name=('row', 'fiber')).sum(axis=0)  21.9 us
    dot_general x2, matrix products, local(): jnp.dot(left_panel, right_panel, precision=lax.Precision.HIGHEST, preferr...  13 us
    reduce_scatter x1, waiting for transfers between devices, local(): lax.psum_scatter(running_sum, 'fiber', scatter_dimension=0, tiled=True)  6.67 us
  transfers between devices with their start and end apart: 5, of which 5 were waited for; matrix products, arithmetic and copies ran while one was open for 4% of the time, Pallas kernels for 0%

profile of v1, /device:TPU:0, one launch (start us, length us, event | category | flops | bytes accessed | tf_op | source)
XLA Modules:
  0.0 229.1 jit_solution(15465286194301561984)
XLA Ops:
  6.5 2.8 %fusion.12 = (f32[192,1,1,768]{3,2,1,0:T(1,128)S(1)}, f32[192,1,1,768]{3,2,1,0:T(1,128)S(1)}) fusion(f32[192,1,2,768]{3,2,1,0:T(2,128)} %param.4), kind=kLoop, calls=%fused_computation.20 | loop fusion | bytes 2359296 | tf_op jit(solution)/shard_map/slice | solution.py:20
  9.3 0.9 copy.14
  10.2 0.0 all-gather.16.cloned.1.call-start
  10.2 0.9 fusion.13
  11.2 0.0 all-gather.10.cloned.1.call-start
  11.3 0.9 copy.13
  12.2 0.0 all-gather.12.cloned.1.call-start
  12.3 0.5 all-gather.12.cloned.1.call-update
  12.8 0.0 reduce-scatter.2.cloned.1.call-start
  12.9 23.0 %all-gather.14.cloned.1.call-done = f32[384,1,1,768]{3,0,2,1:T(8,128)} async-done(((f32[192,1,1,768]{3,0,2,1:T(8,128)}), f32[384,1,1,768]{3,0,2,1:T(8,128)}) %all-gather.14.cloned.1.call-update) | async-done | bytes 1179664 | tf_op jit(solution)/shard_map/all_gather | solution.py:20
  35.8 62.2 %all-gather.16.cloned.1.call-done = f32[1,1,768,1024]{3,2,1,0:T(8,128)} async-done(((f32[1,1,96,1024]{3,2,1,0:T(8,128)}), f32[1,1,768,1024]{3,2,1,0:T(8,128)}) %all-gather.16.cloned.1.call-update) | async-done | bytes 3145744 | tf_op jit(solution)/shard_map/all_gather | solution.py:26
  98.1 0.2 mul.34
  98.2 5.9 %fusion = f32[384,1024]{1,0:T(8,128)S(1)} fusion(f32[1,1,768,1024]{3,2,1,0:T(8,128)} %all-gather.16.cloned.1.call-done, f32[48,8,6,128]{3,2,1,0:T(8,128)S(1)} %bitcast.40, f32[384,1,1,768]{3,0,2,1:T(8,128)S(1)} %copy-done.1), kind=kOutput, calls=%fused_computation | convolution fusion | flops 3624173568 | bytes 7077888 | tf_op jit(solution)/shard_map/dot_general | solution.py:27
  104.2 16.9 %all-gather.10.cloned.1.call-done = f32[384,1,1,768]{3,0,2,1:T(8,128)} async-done(((f32[192,1,1,768]{3,0,2,1:T(8,128)}), f32[384,1,1,768]{3,0,2,1:T(8,128)}) %all-gather.10.cloned.1.call-update) | async-done | bytes 1179664 | tf_op jit(solution)/shard_map/all_gather | solution.py:20
  121.1 62.1 %all-gather.12.cloned.1.call-done = f32[1,1,768,1024]{3,2,1,0:T(8,128)} async-done(((f32[1,1,96,1024]{3,2,1,0:T(8,128)}), f32[1,1,768,1024]{3,2,1,0:T(8,128)}) %all-gather.12.cloned.1.call-update) | async-done | bytes 3145744 | tf_op jit(solution)/shard_map/all_gather | solution.py:26
  183.1 0.2 mul.31
  183.3 7.1 %fusion.4 = f32[384,1024]{1,0:T(8,128)} fusion(f32[384,1024]{1,0:T(8,128)S(1)} %fusion, f32[1,1,768,1024]{3,2,1,0:T(8,128)} %all-gather.12.cloned.1.call-done, f32[48,8,6,128]{3,2,1,0:T(8,128)S(1)} %bitcast.41, f32[384,1,1,768]{3,0,2,1:T(8,128)S(1)} %copy-done.2), kind=kOutput, calls=%fused_computation.5 | convolution fusion | flops 3624566784 | bytes 8650752 | tf_op jit(solution)/shard_map/dot_general | solution.py:27
  190.5 0.7 copy-done.5
  191.1 0.2 broadcast_in_dim.2
  191.3 0.3 copy.29
  191.6 6.7 %reduce-scatter.2.cloned.1.call-done = f32[192,1024]{1,0:T(8,128)} async-done(((f32[384,1024]{1,0:T(8,128)}), f32[192,1024]{1,0:T(8,128)}) %reduce-scatter.2.cloned.1.call-update) | async-done | bytes 786448 | tf_op jit(solution)/shard_map/reduce_scatter | solution.py:40
  198.3 1.3 fusion.11
  199.6 21.9 %all-gather.4 = f32[16384]{0:T(1024)S(1)} all-gather(f32[1024]{0:T(1024)S(1)} %fusion.11), channel_id=6, replica_groups=mesh['row'=8,'col'=2,'fiber'=2] {'row','fiber'}, dimensions={0}, use_global_device_ids=true | all-gather | bytes 69632 | tf_op jit(solution)/shard_map/all_gather | solution.py:45
  221.6 1.0 broadcast_divide_fusion
  (22 shorter events, 0.1 us)
Async XLA Ops:
  6.5 3.7 %copy-start.3 = (f32[1,2,96,1024]{3,2,1,0:T(8,128)S(1)}, f32[1,2,96,1024]{3,2,1,0:T(8,128)}, u32[]{:S(2)}) copy-start(f32[1,2,96,1024]{3,2,1,0:T(8,128)} %param.5) | copy-start | bytes 2359300
  6.5 29.3 %all-gather.14.cloned.1.call-start = ((), (), s32[]{:S(2)}) async-start(), calls=%async_computation.4 | async-start | bytes 1769472 | tf_op jit(solution)/shard_map/all_gather | solution.py:20
  10.2 87.9 %all-gather.16.cloned.1.call-start = ((), (), s32[]{:S(2)}) async-start(), calls=%async_computation.5 | async-start | bytes 3538944 | tf_op jit(solution)/shard_map/all_gather | solution.py:26
  11.2 1.7 copy-start.4
  11.2 109.8 %all-gather.10.cloned.1.call-start = ((), (), s32[]{:S(2)}) async-start(), calls=%async_computation.2 | async-start | bytes 1769472 | tf_op jit(solution)/shard_map/all_gather | solution.py:20
  12.2 170.9 %all-gather.12.cloned.1.call-start = ((), (), s32[]{:S(2)}) async-start(), calls=%async_computation.3 | async-start | bytes 3538944 | tf_op jit(solution)/shard_map/all_gather | solution.py:26
  12.8 185.5 %reduce-scatter.2.cloned.1.call-start = ((), (), s32[]{:S(2)}) async-start(), calls=%async_computation.1 | async-start | bytes 2359296 | tf_op jit(solution)/shard_map/reduce_scatter | solution.py:40
  35.8 62.4 %copy-start.1 = (f32[384,1,1,768]{3,0,2,1:T(8,128)S(1)}, f32[384,1,1,768]{3,0,2,1:T(8,128)}, u32[]{:S(2)}) copy-start(f32[384,1,1,768]{3,0,2,1:T(8,128)} %all-gather.14.cloned.1.call-done) | copy-start | bytes 3538948
  121.1 62.3 %copy-start.2 = (f32[384,1,1,768]{3,0,2,1:T(8,128)S(1)}, f32[384,1,1,768]{3,0,2,1:T(8,128)}, u32[]{:S(2)}) copy-start(f32[384,1,1,768]{3,0,2,1:T(8,128)} %all-gather.10.cloned.1.call-done) | copy-start | bytes 3538948
  190.4 0.7 copy-start.5
  198.3 23.3 %copy-start = (f32[192,1024]{1,0:T(8,128)S(1)}, f32[192,1024]{1,0:T(8,128)}, u32[]{:S(2)}) copy-start(f32[192,1024]{1,0:T(8,128)} %reduce-scatter.2.cloned.1.call-done) | copy-start | bytes 2359300
Sparse Core Ops, SparseCore 0:
  10.3 25.4 all-gather.13
  38.0 60.0 all-gather.15
  99.6 21.4 all-gather.9
  123.1 60.0 all-gather.11
  190.6 7.6 reduce-scatter.1
